TPU v7x, 256 devices: a whole 4x4x8 slice. The times are simulated.
256 devices in a mesh: seq: 32 (over z_hi, x, core), ch: 8 (over z_lo, y).
Axes of the slice: x: 4, y: 4, z: 8 (z_hi: 4, z_lo: 2; z = z_hi * 2 + z_lo), core: 2. Of those that a mesh axis runs over, the one named last changes fastest.
Arguments:
- query_act: bfloat16 [4096, 4096], P('seq', 'ch'), may hold values from -6 to 6
- key_act: bfloat16 [4096, 4096], P('seq', 'ch'), may hold values from -6 to 6
- value_act: bfloat16 [4096, 4096], P('seq', 'ch'), may hold values from -6 to 6
- filter_taps: bfloat16 [4096, 4096], P('seq', 'ch'), may hold values from -2 to 2
- out_grad: bfloat16 [4096, 4096], P('seq', 'ch'), may hold values from -6 to 6
- out_weight: bfloat16 [4096, 4096], P('ch'), may hold values from -0.09375 to 0.09375
Outputs:
- mixed_out: bfloat16 [4096, 4096], P('seq', 'ch')
- query_grad: bfloat16 [4096, 4096], P('seq', 'ch')
- key_grad: bfloat16 [4096, 4096], P('seq', 'ch')
- value_grad: bfloat16 [4096, 4096], P('seq', 'ch')
- filter_grad: float32 [4096, 4096], P('seq', 'ch')
All inputs are finite; a program needn't handle non-finite values.
Results may differ from a plain program's by a relative error of at most 0.02.
Values may be sent and summed in bfloat16 or wider, within the bound.
A program may use at most 128 MiB of HBM per device.

v0:
```python
import math

import jax
import jax.numpy as jnp
from jax import lax
from jax.sharding import PartitionSpec as P


def dft_tables(span_rows):
    period = 2 * span_rows
    frequency = jnp.arange(span_rows, dtype=jnp.int32)
    times_in = jnp.arange(span_rows, dtype=jnp.int32)
    times_out = jnp.arange(period, dtype=jnp.int32)
    parity_in = 1.0 - 2.0 * (times_in % 2).astype(jnp.float32)
    parity_out = 1.0 - 2.0 * (times_out % 2).astype(jnp.float32)
    phase_in = (frequency[:, None] * times_in[None, :] % period).astype(jnp.float32) * (
        2.0 * math.pi / period
    )
    cosine_rows = jnp.cos(phase_in)
    sine_rows = jnp.where(frequency[:, None] == 0, parity_in[None, :], -jnp.sin(phase_in))
    forward_t = jnp.concatenate([cosine_rows, sine_rows], axis=0)
    phase_out = (times_out[:, None] * frequency[None, :] % period).astype(jnp.float32) * (
        2.0 * math.pi / period
    )
    scaling = jnp.where(frequency == 0, 1.0, 2.0).astype(jnp.float32) / period
    cosinus_table_entries = jnp.cos(phase_out) * scaling[None, :]
    sine_cols = jnp.where(
        frequency[None, :] == 0,
        parity_out[:, None] / period,
        -jnp.sin(phase_out) * scaling[None, :],
    )
    inverse_t = jnp.concatenate([cosinus_table_entries, sine_cols], axis=1)
    alternate = 1.0 - 2.0 * (frequency % 2).astype(jnp.float32)
    top_sign = 1.0 - 2.0 * float(span_rows % 2)
    shift_sign = jnp.concatenate([alternate, jnp.where(frequency == 0, top_sign, alternate)])[
        :, None
    ]
    pair_mask = (frequency > 0).astype(jnp.float32)[:, None]
    return (forward_t, inverse_t, shift_sign, pair_mask)


def split_table(forward_t):
    table_high = forward_t.astype(jnp.bfloat16)
    kept_high = lax.optimization_barrier(table_high)
    table_low = (forward_t - kept_high.astype(jnp.float32)).astype(jnp.bfloat16)
    return (table_high, table_low)


def packed_product(first_spec, second_spec, pair_mask, conjugate):
    half_rows = first_spec.shape[-2] // 2
    first_real = first_spec[..., :half_rows, :]
    leading_quadrature_term = first_spec[..., half_rows:, :]
    second_real = second_spec[..., :half_rows, :]
    second_imag = second_spec[..., half_rows:, :]
    cross_real = leading_quadrature_term * second_imag
    if conjugate:
        real_part = first_real * second_real + pair_mask * cross_real
        imag_part = (
            pair_mask * (first_real * second_imag - leading_quadrature_term * second_real)
            + (1.0 - pair_mask) * cross_real
        )
    else:
        real_part = first_real * second_real - pair_mask * cross_real
        imag_part = (
            pair_mask * (first_real * second_imag + leading_quadrature_term * second_real)
            + (1.0 - pair_mask) * cross_real
        )
    return jnp.concatenate([real_part, imag_part], axis=-2)


def grouped_sums(spec_u, spec_h, spec_g, own_index, shift_sign, pair_mask):
    block_count = spec_u.shape[0]
    group_width = 8
    zero_spec = jnp.zeros(spec_u.shape[1:], jnp.float32)

    def fetch(spec, indices, usable):
        picked = spec[jnp.clip(indices, 0, block_count - 1)].astype(jnp.float32)
        return jnp.where(usable[:, None, None], picked, 0.0)

    def group_step(group, carry):
        conv_acc, ugrad_acc, hgrad_acc = carry
        indices = group * group_width + jnp.arange(group_width, dtype=jnp.int32)
        u_now = spec_u[indices].astype(jnp.float32)
        h_now = spec_h[indices].astype(jnp.float32)
        u_prev = fetch(spec_u, indices - 1, indices >= 1)
        lag = own_index - indices
        h_lag = fetch(spec_h, lag, lag >= 0)
        conv_acc = conv_acc + jnp.sum(
            packed_product(u_prev + shift_sign * u_now, h_lag, pair_mask, False), axis=0
        )
        lead = own_index + indices
        g_lead = fetch(spec_g, lead, lead <= block_count - 1)
        g_next = fetch(spec_g, lead + 1, lead + 1 <= block_count - 1)
        ahead = g_lead + shift_sign * g_next
        ugrad_acc = ugrad_acc + jnp.sum(packed_product(h_now, ahead, pair_mask, True), axis=0)
        hgrad_acc = hgrad_acc + jnp.sum(packed_product(u_now, ahead, pair_mask, True), axis=0)
        return (conv_acc, ugrad_acc, hgrad_acc)

    return lax.fori_loop(
        0, block_count // group_width, group_step, (zero_spec, zero_spec, zero_spec)
    )


def transform(blocks, table_high, table_low):
    high_part = jnp.einsum("pt,ntc->npc", table_high, blocks, preferred_element_type=jnp.float32)
    low_part = jnp.einsum("pt,ntc->npc", table_low, blocks, preferred_element_type=jnp.float32)
    return (high_part + low_part).astype(jnp.bfloat16)


def own_block(spec_u, spec_h, spec_g, own_index, inverse_t, shift_sign, pair_mask, span_rows):
    conv_spec, ugrad_spec, hgrad_spec = grouped_sums(
        spec_u, spec_h, spec_g, own_index, shift_sign, pair_mask
    )
    conv = jnp.dot(inverse_t[span_rows:], conv_spec, precision=lax.Precision.HIGHEST)
    u_grad = jnp.dot(inverse_t[:span_rows], ugrad_spec, precision=lax.Precision.HIGHEST)
    filter_grad = jnp.dot(inverse_t[:span_rows], hgrad_spec, precision=lax.Precision.HIGHEST)
    return (conv, u_grad, filter_grad)


def per_device(query_act, key_act, value_act, filter_taps, out_grad, out_weight):
    span_rows, feature_count = query_act.shape
    block_count = lax.axis_size("seq")
    own_index = lax.axis_index("seq")
    forward_t, inverse_t, shift_sign, pair_mask = dft_tables(span_rows)
    table_high, table_low = split_table(forward_t)
    product = (key_act.astype(jnp.float32) * value_act.astype(jnp.float32)).astype(jnp.bfloat16)
    gated_grad = lax.dot_general(
        lax.all_gather(out_grad, "ch", axis=1, tiled=True),
        out_weight,
        (((1,), (1,)), ((), ())),
        preferred_element_type=jnp.float32,
    )
    conv_grad = (gated_grad * query_act.astype(jnp.float32)).astype(jnp.bfloat16)
    own_u = transform(product[None], table_high, table_low)[0]
    own_h = transform(filter_taps[None], table_high, table_low)[0]
    own_g = transform(conv_grad[None], table_high, table_low)[0]
    received = (
        lax.all_gather(own_u, "seq", axis=0, tiled=True),
        lax.all_gather(own_h, "seq", axis=0, tiled=True),
        lax.all_gather(own_g, "seq", axis=0, tiled=True),
    )
    spec_u, spec_h, spec_g = [
        series.reshape(block_count, 2 * span_rows, feature_count) for series in received
    ]
    conv, u_grad, filter_grad = own_block(
        spec_u, spec_h, spec_g, own_index, inverse_t, shift_sign, pair_mask, span_rows
    )
    gated = (query_act.astype(jnp.float32) * conv).astype(jnp.bfloat16)
    partial_out = jnp.dot(gated, out_weight, preferred_element_type=jnp.float32)
    mixed_out = lax.psum_scatter(
        partial_out.astype(jnp.bfloat16), "ch", scatter_dimension=1, tiled=True
    )
    query_grad = (gated_grad * conv).astype(jnp.bfloat16)
    key_grad = (u_grad * value_act.astype(jnp.float32)).astype(jnp.bfloat16)
    value_grad = (u_grad * key_act.astype(jnp.float32)).astype(jnp.bfloat16)
    return (mixed_out, query_grad, key_grad, value_grad, filter_grad)


def solution(mesh):
    return jax.shard_map(
        per_device,
        mesh=mesh,
        in_specs=(
            P("seq", "ch"),
            P("seq", "ch"),
            P("seq", "ch"),
            P("seq", "ch"),
            P("seq", "ch"),
            P("ch", None),
        ),
        out_specs=(P("seq", "ch"), P("seq", "ch"), P("seq", "ch"), P("seq", "ch"), P("seq", "ch")),
        check_vma=False,
    )
```

profile of v0, /device:TPU:1, one launch (start us, length us, event | category | flops | bytes accessed | tf_op | source)
XLA Modules:
  0.0 559.3 jit_solution(4437507908320917075)
XLA Ops:
  8.3 1.2 fusion.43
  9.5 1.9 fusion.19
  11.6 38.6 %all-gather.9.cloned.1.call-done = bf16[128,4096]{1,0:T(8,128)(2,1)} async-done(((bf16[128,512]{1,0:T(8,128)(2,1)}), bf16[128,4096]{1,0:T(8,128)(2,1)}) %all-gather.9.cloned.1.call-update) | async-done | bytes 1048592 | tf_op jit(solution)/shard_map/all_gather | solution.py:128
  50.2 4.0 fusion.62
  57.4 1.2 multiply_select_fusion
  58.7 84.1 %all-gather.11.cloned.1.call-done = bf16[1,8192,512]{1,2,0:T(8,128)(2,1)} async-done(((bf16[1,256,512]{1,2,0:T(8,128)(2,1)}), bf16[1,8192,512]{1,2,0:T(8,128)(2,1)}) %all-gather.11.cloned.1.call-update) | async-done | bytes 8388624 | tf_op jit(solution)/shard_map/all_gather | solution.py:138
  142.8 11.6 %copy.13 = bf16[1,8192,512]{2,1,0:T(8,128)(2,1)} copy(bf16[1,8192,512]{1,2,0:T(8,128)(2,1)} %all-gather.11.cloned.1.call-done) | data formatting | bytes 16777216
  154.5 74.7 %all-gather.13.cloned.1.call-done = bf16[1,8192,512]{1,2,0:T(8,128)(2,1)} async-done(((bf16[1,256,512]{1,2,0:T(8,128)(2,1)}), bf16[1,8192,512]{1,2,0:T(8,128)(2,1)}) %all-gather.13.cloned.1.call-update) | async-done | bytes 8388624 | tf_op jit(solution)/shard_map/all_gather | solution.py:140
  229.1 12.0 %copy.14 = bf16[1,8192,512]{2,1,0:T(8,128)(2,1)} copy(bf16[1,8192,512]{1,2,0:T(8,128)(2,1)} %all-gather.13.cloned.1.call-done) | data formatting | bytes 16777216
  241.2 64.7 %all-gather.7.cloned.1.call-done = bf16[8192,512]{1,0:T(8,128)(2,1)} async-done(((bf16[256,512]{1,0:T(8,128)(2,1)}), bf16[8192,512]{1,0:T(8,128)(2,1)}) %all-gather.7.cloned.1.call-update) | async-done | bytes 8388624 | tf_op jit(solution)/shard_map/all_gather | solution.py:139
  305.8 203.5 %while.21 = (s32[]{:T(128)}, f32[256,512]{1,0:T(8,128)S(1)}, f32[256,512]{1,0:T(8,128)}, f32[256,512]{1,0:T(8,128)}, bf16[32,256,512]{2,1,0:T(8,128)(2,1)}, /*in...) while((s32[]{:T(128)}, f32[256,512]{1,0:T(8,128)S(1)}, ...), condition=%wide.region_4.5_spmd.clone.clone, body=%wide.region_0.4_spmd.clone.clone.sunk | while | flops 38148044 | bytes 155214800 | solution.py:99
  305.9 4.1 gather_fusion
  310.0 2.7 convert_select_fusion.2
  312.7 5.3 gather_fusion.1
  318.1 5.4 gather_fusion.2
  323.5 4.1 gather_fusion.3
  327.6 5.4 gather_fusion.4
  333.0 6.7 %multiply_add_fusion.9 = (f32[8,256,512]{2,1,0:T(8,128)}, f32[8,256,512]{2,1,0:T(8,128)S(1)}) fusion(bf16[8,256,512]{2,1,0:T(8,128)(2,1)} %gather_fusion.1, bf16[8,256,512]{2,1,0:T(8,128)(2,1)} %gather_fusion.2, f32[256]{0:T(256)S(1)} %get-tuple-element.514, pred[8]{0:T(512)(128)(4,1)S(1)} %add_compare_fusion.2, pred[8]{0:T(512)(128)(4,1)S(1)} %fusion.88, ...), kind=kLoop, calls=%fused_computation.11.clone.1 | loop fusion | flops 11534336 | bytes 16778264 | tf_op jit(solution)/shard_map/while/body/eval_jaxpr/add | solution.py:94
  339.7 1.2 multiply_subtract_fusion.2
  341.6 5.4 gather_fusion.5
  347.0 2.2 convert_element_type.325
  349.8 1.6 copy-done.3
  351.4 2.3 multiply_add_fusion.10
  356.8 4.1 gather_fusion
  360.8 2.7 convert_select_fusion.2
  363.6 5.3 gather_fusion.1
  368.9 5.4 gather_fusion.2
  374.4 4.1 gather_fusion.3
  378.5 5.4 gather_fusion.4
  383.8 6.7 %multiply_add_fusion.9 = (f32[8,256,512]{2,1,0:T(8,128)}, f32[8,256,512]{2,1,0:T(8,128)S(1)}) fusion(bf16[8,256,512]{2,1,0:T(8,128)(2,1)} %gather_fusion.1, bf16[8,256,512]{2,1,0:T(8,128)(2,1)} %gather_fusion.2, f32[256]{0:T(256)S(1)} %get-tuple-element.514, pred[8]{0:T(512)(128)(4,1)S(1)} %add_compare_fusion.2, pred[8]{0:T(512)(128)(4,1)S(1)} %fusion.88, ...), kind=kLoop, calls=%fused_computation.11.clone.1 | loop fusion | flops 11534336 | bytes 16778264 | tf_op jit(solution)/shard_map/while/body/eval_jaxpr/add | solution.py:94
  390.6 1.2 multiply_subtract_fusion.2
  392.4 5.4 gather_fusion.5
  397.9 2.2 convert_element_type.325
  400.6 1.6 copy-done.3
  402.2 2.3 multiply_add_fusion.10
  407.6 4.1 gather_fusion
  411.7 2.7 convert_select_fusion.2
  414.4 5.3 gather_fusion.1
  419.8 5.4 gather_fusion.2
  425.2 4.1 gather_fusion.3
  429.3 5.4 gather_fusion.4
  434.7 6.7 %multiply_add_fusion.9 = (f32[8,256,512]{2,1,0:T(8,128)}, f32[8,256,512]{2,1,0:T(8,128)S(1)}) fusion(bf16[8,256,512]{2,1,0:T(8,128)(2,1)} %gather_fusion.1, bf16[8,256,512]{2,1,0:T(8,128)(2,1)} %gather_fusion.2, f32[256]{0:T(256)S(1)} %get-tuple-element.514, pred[8]{0:T(512)(128)(4,1)S(1)} %add_compare_fusion.2, pred[8]{0:T(512)(128)(4,1)S(1)} %fusion.88, ...), kind=kLoop, calls=%fused_computation.11.clone.1 | loop fusion | flops 11534336 | bytes 16778264 | tf_op jit(solution)/shard_map/while/body/eval_jaxpr/add | solution.py:94
  441.4 1.2 multiply_subtract_fusion.2
  443.3 5.4 gather_fusion.5
  448.7 2.2 convert_element_type.325
  451.5 1.6 copy-done.3
  453.1 2.3 multiply_add_fusion.10
  458.5 4.1 gather_fusion
  462.6 2.7 convert_select_fusion.2
  465.3 5.3 gather_fusion.1
  470.6 5.4 gather_fusion.2
  476.1 4.1 gather_fusion.3
  480.2 5.4 gather_fusion.4
  485.6 6.7 %multiply_add_fusion.9 = (f32[8,256,512]{2,1,0:T(8,128)}, f32[8,256,512]{2,1,0:T(8,128)S(1)}) fusion(bf16[8,256,512]{2,1,0:T(8,128)(2,1)} %gather_fusion.1, bf16[8,256,512]{2,1,0:T(8,128)(2,1)} %gather_fusion.2, f32[256]{0:T(256)S(1)} %get-tuple-element.514, pred[8]{0:T(512)(128)(4,1)S(1)} %add_compare_fusion.2, pred[8]{0:T(512)(128)(4,1)S(1)} %fusion.88, ...), kind=kLoop, calls=%fused_computation.11.clone.1 | loop fusion | flops 11534336 | bytes 16778264 | tf_op jit(solution)/shard_map/while/body/eval_jaxpr/add | solution.py:94
  492.3 1.2 multiply_subtract_fusion.2
  494.1 5.4 gather_fusion.5
  499.6 2.2 convert_element_type.325
  502.3 1.6 copy-done.3
  503.9 2.3 multiply_add_fusion.10
  509.3 1.9 multiply_convert_fusion
  511.2 4.0 convolution_convert_fusion
  515.3 1.1 fusion.46
  516.5 1.1 fusion.22
  517.6 35.1 %reduce-scatter.2.cloned.1.call-done = bf16[128,512]{1,0:T(8,128)(2,1)} async-done(((bf16[128,4096]{1,0:T(8,128)(2,1)}), bf16[128,512]{1,0:T(8,128)(2,1)}) %reduce-scatter.2.cloned.1.call-update) | async-done | bytes 131088 | tf_op jit(solution)/shard_map/reduce_scatter | solution.py:150
  (182 shorter events, 21.7 us)
Async XLA Ops:
  7.2 48.8 %copy-start = (bf16[128,512]{1,0:T(8,128)(2,1)S(1)}, bf16[128,512]{1,0:T(8,128)(2,1)}, u32[]{:S(2)}) copy-start(bf16[128,512]{1,0:T(8,128)(2,1)} %param.11) | copy-start | bytes 393220
  7.2 43.0 %all-gather.9.cloned.1.call-start = ((), (), s32[]{:S(2)}) async-start(), calls=%async_computation.2 | async-start | bytes 1179648 | tf_op jit(solution)/shard_map/all_gather | solution.py:128
  7.9 134.9 %all-gather.11.cloned.1.call-start = ((), (), s32[]{:S(2)}) async-start(), calls=%async_computation.4 | async-start | bytes 8650752 | tf_op jit(solution)/shard_map/all_gather | solution.py:138
  11.5 42.7 %copy-start.15 = (bf16[128,512]{1,0:T(8,128)(2,1)S(1)}, bf16[128,512]{1,0:T(8,128)(2,1)}, u32[]{:S(2)}) copy-start(bf16[128,512]{1,0:T(8,128)(2,1)} %param.8) | copy-start | bytes 393220
  11.5 217.6 %all-gather.13.cloned.1.call-start = ((), (), s32[]{:S(2)}) async-start(), calls=%async_computation.5 | async-start | bytes 8650752 | tf_op jit(solution)/shard_map/all_gather | solution.py:140
  54.2 0.7 copy-start.10
  55.9 249.9 %all-gather.7.cloned.1.call-start = ((), (), s32[]{:S(2)}) async-start(), calls=%async_computation.1 | async-start | bytes 8650752 | tf_op jit(solution)/shard_map/all_gather | solution.py:139
  57.1 495.6 %reduce-scatter.2.cloned.1.call-start = ((), (), s32[]{:S(2)}) async-start(), calls=%async_computation.3 | async-start | bytes 1179648 | tf_op jit(solution)/shard_map/reduce_scatter | solution.py:150
  305.8 203.5 %copy-start.11 = (f32[128,512]{1,0:T(8,128)S(1)}, f32[128,512]{1,0:T(8,128)}, u32[]{:S(2)}) copy-start(f32[128,512]{1,0:T(8,128)} %copy-done.10) | copy-start | bytes 786436
  305.8 203.5 %copy-start.12 = (f32[256,128]{1,0:T(8,128)S(1)}, f32[256,128]{1,0:T(8,128)}, u32[]{:S(2)}) copy-start(f32[256,128]{1,0:T(8,128)} %get-tuple-element.404) | copy-start | bytes 393220
  333.0 6.7 %copy-start.2 = (f32[8,256,512]{2,1,0:T(8,128)S(1)}, f32[8,256,512]{2,1,0:T(8,128)}, u32[]{:S(2)}) copy-start(f32[8,256,512]{2,1,0:T(8,128)} %convert_select_fusion.2) | copy-start | bytes 12582916 | tf_op jit(solution)/shard_map/while
  349.2 2.2 copy-start.3
  354.2 1.0 copy-start.4
  354.2 1.2 copy-start.7
  355.8 0.8 copy-start.5
  355.8 1.0 copy-start.8
  383.8 6.7 %copy-start.2 = (f32[8,256,512]{2,1,0:T(8,128)S(1)}, f32[8,256,512]{2,1,0:T(8,128)}, u32[]{:S(2)}) copy-start(f32[8,256,512]{2,1,0:T(8,128)} %convert_select_fusion.2) | copy-start | bytes 12582916 | tf_op jit(solution)/shard_map/while
  400.0 2.2 copy-start.3
  405.1 1.0 copy-start.4
  405.1 1.2 copy-start.7
  406.6 0.8 copy-start.5
  406.6 1.0 copy-start.8
  434.7 6.7 %copy-start.2 = (f32[8,256,512]{2,1,0:T(8,128)S(1)}, f32[8,256,512]{2,1,0:T(8,128)}, u32[]{:S(2)}) copy-start(f32[8,256,512]{2,1,0:T(8,128)} %convert_select_fusion.2) | copy-start | bytes 12582916 | tf_op jit(solution)/shard_map/while
  450.9 2.2 copy-start.3
  455.9 1.0 copy-start.4
  455.9 1.2 copy-start.7
  457.5 0.8 copy-start.5
  457.5 1.0 copy-start.8
  485.6 6.7 %copy-start.2 = (f32[8,256,512]{2,1,0:T(8,128)S(1)}, f32[8,256,512]{2,1,0:T(8,128)}, u32[]{:S(2)}) copy-start(f32[8,256,512]{2,1,0:T(8,128)} %convert_select_fusion.2) | copy-start | bytes 12582916 | tf_op jit(solution)/shard_map/while
  501.8 2.2 copy-start.3
  506.8 1.0 copy-start.4
  506.8 1.2 copy-start.7
  508.3 0.8 copy-start.5
  508.3 1.0 copy-start.8
  511.2 4.1 copy-start.9
  511.2 4.1 copy-start.13
  511.2 4.1 copy-start.14
  511.2 41.5 %copy-start.1 = (bf16[128,512]{1,0:T(8,128)(2,1)S(1)}, bf16[128,512]{1,0:T(8,128)(2,1)}, u32[]{:S(2)}) copy-start(bf16[128,512]{1,0:T(8,128)(2,1)} %param.11) | copy-start | bytes 393220
  515.3 1.2 copy-start.6
  515.3 1.2 copy-start.16
  515.3 1.2 copy-start.17
Sparse Core Ops, SparseCore 0:
  9.8 40.2 all-gather.8
  52.6 90.1 all-gather.10
  145.3 83.7 all-gather.12
  231.5 74.2 all-gather.6
  515.4 37.2 reduce-scatter.1
where the time goes:
time: 565 us; the launch traced here: 559 us
  waiting for transfers between devices  298 us (53%)
  local copies, waits for them, and re-layouts  156 us (28%)
  other arithmetic  72.6 us (13%)
  matrix products  17.8 us (3%)
  between operations  14 us (2%)
    all_gather x1, waiting for transfers between devices, per_device(): lax.all_gather(own_u, 'seq', axis=0, tiled=True)  84.1 us
    gather x16, local copies, waits for them, and re-layouts, fetch(): picked = spec[jnp.clip(indices, 0, block_count - 1)].astype(jnp.float32)  80.8 us
    all_gather x1, waiting for transfers between devices, per_device(): lax.all_gather(own_g, 'seq', axis=0, tiled=True)  74.7 us
    all_gather x1, waiting for transfers between devices, per_device(): lax.all_gather(own_h, 'seq', axis=0, tiled=True)  64.7 us
    all_gather x1, waiting for transfers between devices, per_device(): lax.all_gather(out_grad, 'ch', axis=1, tiled=True)  38.6 us
    reduce_scatter x1, waiting for transfers between devices, per_device(): lax.psum_scatter(partial_out.astype(jnp.bfloat16), 'ch', scatter_dimensio...  35.1 us
    add x4, other arithmetic, group_step(): ahead = g_lead + shift_sign * g_next  26.7 us
    unnamed x26, local copies, waits for them, and re-layouts  24.2 us
  transfers between devices with their start and end apart: 5, of which 5 were waited for; matrix products, arithmetic and copies ran while one was open for 7% of the time, Pallas kernels for 0%

commit v1 on v0

v1 whole, which is shorter than its diff:
```python
import functools
import math

import jax
import jax.numpy as jnp
import numpy as np
from jax import lax
from jax.experimental import pallas as pl
from jax.experimental.pallas import tpu as pltpu
from jax.sharding import PartitionSpec as P

MESH = pl.DeviceIdType.MESH
F32 = jnp.float32
BF16 = jnp.bfloat16


def transform_tables(block_count, span_rows, own_channels):
    blocks = np.arange(block_count)
    times = np.arange(span_rows)
    across = 2.0 * math.pi * np.outer(2 * blocks + 1, blocks) / (4 * block_count)
    turn = 2.0 * math.pi * np.outer(2 * blocks + 1, times) / (4 * block_count * span_rows)
    within = 2.0 * math.pi * (np.outer(times, times) % span_rows) / span_rows
    each = np.eye(own_channels)
    across_fwd = np.concatenate([np.kron(np.cos(across), each), np.kron(-np.sin(across), each)], axis=0)
    across_inv = across_fwd.T / (block_count * span_rows)
    within_fwd = np.block([[np.cos(within), -np.sin(within)], [np.sin(within), np.cos(within)]])
    turn_cos = np.repeat(np.cos(turn), own_channels, axis=0)
    turn_sin = np.repeat(np.sin(turn), own_channels, axis=0)
    return (
        jnp.asarray(across_fwd, BF16),
        jnp.asarray(across_inv, BF16),
        jnp.asarray(within_fwd, BF16),
        jnp.asarray(within_fwd.T, BF16),
        jnp.asarray(turn_cos, F32),
        jnp.asarray(turn_sin, F32),
    )


def layer_kernel(
    n_seq,
    n_ch,
    q_ref,
    k_ref,
    v_ref,
    h_ref,
    og_ref,
    w_hbm,
    kf_hbm,
    ki_hbm,
    df_hbm,
    di_hbm,
    tc_hbm,
    ts_hbm,
    mixed_ref,
    qg_ref,
    kg_ref,
    vg_ref,
    fg_ref,
    w,
    kf,
    ki,
    df,
    di,
    tc,
    ts,
    uh_src,
    uh,
    cv_src,
    cv,
    g_src,
    g,
    dd_src,
    dd,
    og,
    rs_src,
    rs,
    level,
    spec_uh,
    spec_out,
    turned,
    gg,
    own_part,
    load_sem,
    send_sem,
    recv_sem,
    ag_send,
    ag_recv,
    rs_send,
    rs_recv,
):
    seq = lax.axis_index("seq")
    ch = lax.axis_index("ch")
    rows, width = q_ref.shape
    lanes = rows
    half = n_seq * (width // n_seq)
    part = width
    step_rows = min(128, half)

    loads = [
        pltpu.make_async_copy(src, dst, load_sem.at[i])
        for i, (src, dst) in enumerate(
            [(kf_hbm, kf), (ki_hbm, ki), (df_hbm, df), (di_hbm, di), (tc_hbm, tc), (ts_hbm, ts), (w_hbm, w)]
        )
    ]
    for load in loads:
        load.start()

    barrier = pltpu.get_barrier_semaphore()

    def greet_seq(i, carry):
        pl.semaphore_signal(
            barrier, inc=1, device_id={"seq": lax.rem(seq + i, n_seq)}, device_id_type=MESH
        )
        return carry

    def greet_ch(i, carry):
        pl.semaphore_signal(
            barrier, inc=1, device_id={"ch": lax.rem(ch + i, n_ch)}, device_id_type=MESH
        )
        return carry

    lax.fori_loop(1, n_seq, greet_seq, 0)
    lax.fori_loop(1, n_ch, greet_ch, 0)

    u = (k_ref[...].astype(F32) * v_ref[...].astype(F32)).astype(BF16)
    uh_src[:, :, :lanes] = u.T.reshape(n_seq, width // n_seq, rows)
    uh_src[:, :, lanes:] = h_ref[...].T.reshape(n_seq, width // n_seq, rows)

    pl.semaphore_wait(barrier, n_seq + n_ch - 2)

    def exchange(src, dst, slot):
        def one(i, carry):
            peer = lax.rem(seq + i, n_seq)
            pltpu.make_async_remote_copy(
                src_ref=src.at[peer],
                dst_ref=dst.at[seq],
                send_sem=send_sem.at[slot],
                recv_sem=recv_sem.at[slot],
                device_id={"seq": peer},
                device_id_type=MESH,
            ).start()
            return carry

        lax.fori_loop(1, n_seq, one, 0)
        dst[seq] = src[seq]

    def arrived(dst, slot):
        landed = dst.at[pl.ds(0, n_seq - 1)]
        pltpu.make_async_copy(landed, landed, recv_sem.at[slot]).wait()

    def departed(src, slot):
        left = src.at[pl.ds(0, n_seq - 1)]
        pltpu.make_async_copy(left, left, send_sem.at[slot]).wait()

    def gather_copy(d):
        peer = lax.rem(ch + d, n_ch)
        return pltpu.make_async_remote_copy(
            src_ref=og_ref,
            dst_ref=og.at[ch],
            send_sem=ag_send.at[d],
            recv_sem=ag_recv.at[d],
            device_id={"ch": peer},
            device_id_type=MESH,
        )

    exchange(uh_src, uh, 0)
    for d in range(1, n_ch):
        gather_copy(d).start()

    for load in loads[:-1]:
        load.wait()

    def forward(values, count, put):
        level[:, : count * lanes] = jnp.dot(kf[...], values, preferred_element_type=F32)
        for r in range(0, half, step_rows):
            c, s = tc[r : r + step_rows, :], ts[r : r + step_rows, :]
            for a in range(count):
                re = level[r : r + step_rows, a * lanes : (a + 1) * lanes]
                im = level[half + r : half + r + step_rows, a * lanes : (a + 1) * lanes]
                z = jnp.concatenate([re * c + im * s, im * c - re * s], axis=1).astype(BF16)
                put(r, a, jnp.dot(z, df[...], preferred_element_type=F32))

    def inverse(product, count, dst):
        for r in range(0, half, step_rows):
            c, s = tc[r : r + step_rows, :], ts[r : r + step_rows, :]
            for a in range(count):
                x = jnp.dot(product(r, a), di[...], preferred_element_type=F32)
                re, im = x[:, :lanes], x[:, lanes:]
                turned[r : r + step_rows, a * lanes : (a + 1) * lanes] = (re * c - im * s).astype(BF16)
                turned[half + r : half + r + step_rows, a * lanes : (a + 1) * lanes] = (
                    im * c + re * s
                ).astype(BF16)
        y = jnp.dot(ki[...], turned[:, : count * lanes], preferred_element_type=F32)
        dst[...] = y.astype(BF16).reshape(dst.shape)

    def put_uh(r, a, value):
        spec_uh[a, r : r + step_rows, :] = value

    def conv_product(r, a):
        x, y = spec_uh[0, r : r + step_rows, :], spec_uh[1, r : r + step_rows, :]
        xr, xi, yr, yi = x[:, :lanes], x[:, lanes:], y[:, :lanes], y[:, lanes:]
        return jnp.concatenate([xr * yr - xi * yi, xr * yi + xi * yr], axis=1).astype(BF16)

    arrived(uh, 0)
    forward(uh[...].reshape(half, 2 * lanes), 2, put_uh)
    inverse(conv_product, 1, cv_src)
    exchange(cv_src, cv, 1)

    loads[-1].wait()

    def grad_block(value, source):
        columns = pl.ds(pl.multiple_of(source * part, part), part)
        return lax.dot_general(value, w[:, columns], (((1,), (1,)), ((), ())), preferred_element_type=F32)

    gg[...] = grad_block(og_ref[...], ch)
    for d in range(1, n_ch):
        gather_copy(d).wait_recv()
        source = lax.rem(ch + n_ch - d, n_ch)
        gg[...] += grad_block(og[source], source)
    conv_grad = (gg[...] * q_ref[...].astype(F32)).astype(BF16)
    g_src[...] = conv_grad.T.reshape(g_src.shape)
    exchange(g_src, g, 2)

    arrived(cv, 1)
    conv = cv[...].reshape(width, rows).T.astype(F32)
    qg_ref[...] = (gg[...] * conv).astype(BF16)
    gated = (q_ref[...].astype(F32) * conv).astype(BF16)

    def scatter_copy(d):
        peer = lax.rem(ch + d, n_ch)
        return pltpu.make_async_remote_copy(
            src_ref=rs_src.at[d],
            dst_ref=rs.at[d],
            send_sem=rs_send.at[d],
            recv_sem=rs_recv.at[d],
            device_id={"ch": peer},
            device_id_type=MESH,
        )

    def out_block(target):
        columns = pl.ds(pl.multiple_of(target * part, part), part)
        return jnp.dot(gated, w[:, columns], preferred_element_type=F32)

    for d in range(1, n_ch):
        rs_src[d] = out_block(lax.rem(ch + d, n_ch)).astype(BF16)
        scatter_copy(d).start()
    own_part[...] = out_block(ch)

    def put_g(r, a, value):
        gr, gi = value[:, :lanes], value[:, lanes:]
        for b in range(2):
            x = spec_uh[1 - b, r : r + step_rows, :]
            xr, xi = x[:, :lanes], x[:, lanes:]
            spec_out[b, r : r + step_rows, :] = jnp.concatenate(
                [xr * gr + xi * gi, xr * gi - xi * gr], axis=1
            ).astype(BF16)

    arrived(g, 2)
    forward(g[...].reshape(half, lanes), 1, put_g)
    inverse(lambda r, a: spec_out[a, r : r + step_rows, :], 2, dd_src)
    exchange(dd_src, dd, 3)

    total = own_part[...]
    for d in range(1, n_ch):
        scatter_copy(d).wait_recv()
        total = total + rs[d].astype(F32)
    mixed_ref[...] = total.astype(BF16)

    arrived(dd, 3)
    u_grad = dd[:, :, :lanes].reshape(width, rows).T.astype(F32)
    kg_ref[...] = (u_grad * v_ref[...].astype(F32)).astype(BF16)
    vg_ref[...] = (u_grad * k_ref[...].astype(F32)).astype(BF16)
    fg_ref[...] = dd[:, :, lanes:].reshape(width, rows).T.astype(F32)

    departed(uh_src, 0)
    departed(cv_src, 1)
    departed(g_src, 2)
    departed(dd_src, 3)
    for d in range(1, n_ch):
        gather_copy(d).wait_send()
        scatter_copy(d).wait_send()


def per_device(query_act, key_act, value_act, filter_taps, out_grad, out_weight):
    rows, width = query_act.shape
    n_seq, n_ch = lax.axis_size("seq"), lax.axis_size("ch")
    own = width // n_seq
    tables = transform_tables(n_seq, rows, own)
    half = n_seq * own
    vmem, anywhere = pl.BlockSpec(memory_space=pltpu.VMEM), pl.BlockSpec(memory_space=pl.ANY)
    bf = jax.ShapeDtypeStruct((rows, width), BF16)

    def blocks(lanes):
        return pltpu.VMEM((n_seq, own, lanes), BF16)

    return pl.pallas_call(
        functools.partial(layer_kernel, n_seq, n_ch),
        out_shape=(bf, bf, bf, bf, jax.ShapeDtypeStruct((rows, width), F32)),
        in_specs=[vmem] * 5 + [anywhere] * 7,
        out_specs=(vmem,) * 5,
        scratch_shapes=[
            pltpu.VMEM(out_weight.shape, BF16),
            *[pltpu.VMEM(t.shape, t.dtype) for t in tables],
            blocks(2 * rows),
            blocks(2 * rows),
            blocks(rows),
            blocks(rows),
            blocks(rows),
            blocks(rows),
            blocks(2 * rows),
            blocks(2 * rows),
            pltpu.VMEM((n_ch, rows, width), BF16),
            pltpu.VMEM((n_ch, rows, width), BF16),
            pltpu.VMEM((n_ch, rows, width), BF16),
            pltpu.VMEM((2 * half, 2 * rows), F32),
            pltpu.VMEM((2, half, 2 * rows), F32),
            pltpu.VMEM((2, half, 2 * rows), BF16),
            pltpu.VMEM((2 * half, 2 * rows), BF16),
            pltpu.VMEM((rows, width), F32),
            pltpu.VMEM((rows, width), F32),
            pltpu.SemaphoreType.DMA((7,)),
            pltpu.SemaphoreType.DMA((4,)),
            pltpu.SemaphoreType.DMA((4,)),
            pltpu.SemaphoreType.DMA((n_ch,)),
            pltpu.SemaphoreType.DMA((n_ch,)),
            pltpu.SemaphoreType.DMA((n_ch,)),
            pltpu.SemaphoreType.DMA((n_ch,)),
        ],
        compiler_params=pltpu.CompilerParams(
            collective_id=0, has_side_effects=True, vmem_limit_bytes=48 * 1024 * 1024
        ),
    )(query_act, key_act, value_act, filter_taps, out_grad, out_weight, *tables)


def solution(mesh):
    return jax.shard_map(
        per_device,
        mesh=mesh,
        in_specs=(P("seq", "ch"),) * 5 + (P("ch", None),),
        out_specs=(P("seq", "ch"),) * 5,
        check_vma=False,
    )
```

time: 565 us -> 74.9 us (0.13)
  the two profiles are of different devices: /device:TPU:1 before, /device:TPU:25 now
where the time goes in v1:
time: 74.9 us; the launch traced here: 74.6 us
  Pallas kernels  59.9 us (80%)
  local copies, waits for them, and re-layouts  14 us (19%)
    pallas_call x1, Pallas kernels, per_device(): pl.pallas_call(functools.partial(layer_kernel, n_seq, n_ch), out_shape=(b...  59.9 us
    unnamed x27, local copies, waits for them, and re-layouts  14 us

profile of v1, /device:TPU:25, one launch (start us, length us, event | category | flops | bytes accessed | tf_op | source)
XLA Modules:
  0.0 74.6 jit_solution(9126938923173134232)
XLA Ops:
  0.6 0.0 copy-start
  0.6 1.2 %copy-done = bf16[512,1024]{1,0:T(8,128)(2,1)S(1)} copy-done((bf16[512,1024]{1,0:T(8,128)(2,1)S(1)}, bf16[512,1024]{1,0:T(8,128)(2,1)}, u32[]{:S(2)}) %copy-start) | copy-done | bytes 1048600
  1.9 0.0 copy-start.1
  1.9 1.2 %copy-done.1 = bf16[1024,512]{1,0:T(8,128)(2,1)S(1)} copy-done((bf16[1024,512]{1,0:T(8,128)(2,1)S(1)}, bf16[1024,512]{1,0:T(8,128)(2,1)}, u32[]{:S(2)}) %copy-start.1) | copy-done | bytes 1048600
  3.1 0.0 copy-start.2
  3.1 0.9 %copy-done.2 = f32[512,128]{1,0:T(8,128)S(1)} copy-done((f32[512,128]{1,0:T(8,128)S(1)}, f32[512,128]{1,0:T(8,128)}, u32[]{:S(2)}) %copy-start.2) | copy-done | bytes 262168
  4.0 0.0 copy-start.3
  4.0 0.9 %copy-done.3 = f32[512,128]{1,0:T(8,128)S(1)} copy-done((f32[512,128]{1,0:T(8,128)S(1)}, f32[512,128]{1,0:T(8,128)}, u32[]{:S(2)}) %copy-start.3) | copy-done | bytes 262168
  5.0 0.0 copy-start.4
  5.0 0.9 %copy-done.4 = bf16[128,512]{1,0:T(8,128)(2,1)S(1)} copy-done((bf16[128,512]{1,0:T(8,128)(2,1)S(1)}, bf16[128,512]{1,0:T(8,128)(2,1)}, u32[]{:S(2)}) %copy-start.4) | copy-done | bytes 131096
  5.9 0.0 copy-start.5
  5.9 0.9 %copy-done.5 = bf16[128,512]{1,0:T(8,128)(2,1)S(1)} copy-done((bf16[128,512]{1,0:T(8,128)(2,1)S(1)}, bf16[128,512]{1,0:T(8,128)(2,1)}, u32[]{:S(2)}) %copy-start.5) | copy-done | bytes 131096
  6.8 0.0 copy-start.6
  6.8 0.9 %copy-done.6 = bf16[128,512]{1,0:T(8,128)(2,1)S(1)} copy-done((bf16[128,512]{1,0:T(8,128)(2,1)S(1)}, bf16[128,512]{1,0:T(8,128)(2,1)}, u32[]{:S(2)}) %copy-start.6) | copy-done | bytes 131096
  7.7 0.0 copy-start.7
  7.7 0.9 %copy-done.7 = bf16[128,512]{1,0:T(8,128)(2,1)S(1)} copy-done((bf16[128,512]{1,0:T(8,128)(2,1)S(1)}, bf16[128,512]{1,0:T(8,128)(2,1)}, u32[]{:S(2)}) %copy-start.7) | copy-done | bytes 131096
  8.6 0.0 copy-start.8
  8.6 0.9 %copy-done.8 = bf16[128,512]{1,0:T(8,128)(2,1)S(1)} copy-done((bf16[128,512]{1,0:T(8,128)(2,1)S(1)}, bf16[128,512]{1,0:T(8,128)(2,1)}, u32[]{:S(2)}) %copy-start.8) | copy-done | bytes 131096
  9.5 0.0 copy-start.9
  9.5 0.9 %copy-done.9 = bf16[256,256]{1,0:T(8,128)(2,1)S(1)} copy-done((bf16[256,256]{1,0:T(8,128)(2,1)S(1)}, bf16[256,256]{1,0:T(8,128)(2,1)}, u32[]{:S(2)}) %copy-start.9) | copy-done | bytes 131096
  10.4 0.0 copy-start.10
  10.4 0.9 %copy-done.10 = bf16[256,256]{1,0:T(8,128)(2,1)S(1)} copy-done((bf16[256,256]{1,0:T(8,128)(2,1)S(1)}, bf16[256,256]{1,0:T(8,128)(2,1)}, u32[]{:S(2)}) %copy-start.10) | copy-done | bytes 131096
  11.3 59.9 %shard_map.155 = (bf16[128,512]{1,0:T(8,128)(2,1)S(1)}, bf16[128,512]{1,0:T(8,128)(2,1)S(1)}, bf16[128,512]{1,0:T(8,128)(2,1)S(1)}, bf16[128,512]{1,0:T(8,128)(2,1)S(1)}, f32[128,512]{1,0:T(8,128)S(1)}) custom-call(bf16[128,512]{1,0:T(8,128)(2,1)S(1)} %copy-done.4, bf16[128,512]{1,0:T(8,128)(2,1)S(1)} %copy-done.5, bf16[128,512]{1,0:T(8,128)(2,1)S(1)} %copy-done.6, ...), custom_call_target="tpu_custom_call" | custom-call | tf_op jit(solution)/shard_map/pallas_call | solution.py:296
  71.3 0.7 copy.22
  71.9 0.7 copy.23
  72.6 0.7 copy.24
  73.2 0.7 copy.25
  73.9 0.7 copy.26
Async XLA Ops:
  0.6 1.2 %copy-start = (bf16[512,1024]{1,0:T(8,128)(2,1)S(1)}, bf16[512,1024]{1,0:T(8,128)(2,1)}, u32[]{:S(2)}) copy-start(bf16[512,1024]{1,0:T(8,128)(2,1)} %constant.13.clone.ki_hbm) | copy-start | bytes 3145732
  1.9 1.2 %copy-start.1 = (bf16[1024,512]{1,0:T(8,128)(2,1)S(1)}, bf16[1024,512]{1,0:T(8,128)(2,1)}, u32[]{:S(2)}) copy-start(bf16[1024,512]{1,0:T(8,128)(2,1)} %constant.12.clone.kf_hbm) | copy-start | bytes 3145732
  3.1 0.9 %copy-start.2 = (f32[512,128]{1,0:T(8,128)S(1)}, f32[512,128]{1,0:T(8,128)}, u32[]{:S(2)}) copy-start(f32[512,128]{1,0:T(8,128)} %constant.17.clone.ts_hbm) | copy-start | bytes 786436
  4.0 0.9 %copy-start.3 = (f32[512,128]{1,0:T(8,128)S(1)}, f32[512,128]{1,0:T(8,128)}, u32[]{:S(2)}) copy-start(f32[512,128]{1,0:T(8,128)} %constant.16.clone.tc_hbm) | copy-start | bytes 786436
  5.0 0.9 %copy-start.4 = (bf16[128,512]{1,0:T(8,128)(2,1)S(1)}, bf16[128,512]{1,0:T(8,128)(2,1)}, u32[]{:S(2)}) copy-start(bf16[128,512]{1,0:T(8,128)(2,1)} %q_ref.1) | copy-start | bytes 393220
  5.9 0.9 %copy-start.5 = (bf16[128,512]{1,0:T(8,128)(2,1)S(1)}, bf16[128,512]{1,0:T(8,128)(2,1)}, u32[]{:S(2)}) copy-start(bf16[128,512]{1,0:T(8,128)(2,1)} %k_ref.1) | copy-start | bytes 393220
  6.8 0.9 %copy-start.6 = (bf16[128,512]{1,0:T(8,128)(2,1)S(1)}, bf16[128,512]{1,0:T(8,128)(2,1)}, u32[]{:S(2)}) copy-start(bf16[128,512]{1,0:T(8,128)(2,1)} %v_ref.1) | copy-start | bytes 393220
  7.7 0.9 %copy-start.7 = (bf16[128,512]{1,0:T(8,128)(2,1)S(1)}, bf16[128,512]{1,0:T(8,128)(2,1)}, u32[]{:S(2)}) copy-start(bf16[128,512]{1,0:T(8,128)(2,1)} %h_ref.1) | copy-start | bytes 393220
  8.6 0.9 %copy-start.8 = (bf16[128,512]{1,0:T(8,128)(2,1)S(1)}, bf16[128,512]{1,0:T(8,128)(2,1)}, u32[]{:S(2)}) copy-start(bf16[128,512]{1,0:T(8,128)(2,1)} %og_ref.1) | copy-start | bytes 393220
  9.5 0.9 %copy-start.9 = (bf16[256,256]{1,0:T(8,128)(2,1)S(1)}, bf16[256,256]{1,0:T(8,128)(2,1)}, u32[]{:S(2)}) copy-start(bf16[256,256]{1,0:T(8,128)(2,1)} %constant.15.clone.di_hbm) | copy-start | bytes 393220
  10.4 0.9 %copy-start.10 = (bf16[256,256]{1,0:T(8,128)(2,1)S(1)}, bf16[256,256]{1,0:T(8,128)(2,1)}, u32[]{:S(2)}) copy-start(bf16[256,256]{1,0:T(8,128)(2,1)} %constant.14.clone.df_hbm) | copy-start | bytes 393220

commit v2 on v1

v2 whole, which is shorter than its diff:
```python
import functools
import math

import jax
import jax.numpy as jnp
import numpy as np
from jax import lax
from jax.experimental import pallas as pl
from jax.experimental.pallas import tpu as pltpu
from jax.sharding import PartitionSpec as P

MESH = pl.DeviceIdType.MESH
F32 = jnp.float32
BF16 = jnp.bfloat16


NEAR = ((0, 1), (0, -1))
GATHER_ROUTES = ((1, 0), (0, 2)) + NEAR + NEAR + ((1, 0),)
GATHER_BLOCKS = ((0, 0),) * 4 + ((1, 0), (1, 0), (0, 2))
GATHER_PASSED = ((0, (4, 5)), (1, (6,)))
GATHER_SOURCES = ((1, 0), (0, 2), (0, -1), (0, 1), (1, -1), (1, 1), (1, 2))
GATHER_ORDER = (0, 1, 2, 3, 4, 5, 6)
SCATTER_ROUTES = ((1, 0),) + NEAR + NEAR + ((0, 2), (1, 0))
SCATTER_BLOCKS = ((1, 2), (1, 1), (1, -1), (0, 1), (0, -1), (0, 2), (1, 0))
SCATTER_ADDS = ((), (), (), (), (), (0,), (1, 2))
GREETED = ((1, 0), (0, 2)) + NEAR


def peers_far_first(seq, n_seq):
    if n_seq < 32:
        return [(seq + i) % n_seq for i in range(1, n_seq)]
    z_now, x_now, core_now = seq // 8, seq // 2 % 4, seq % 2
    z = [(z_now + d) % 4 * 8 for d in range(4)]
    x = [(x_now + d) % 4 * 2 for d in range(4)]
    core = [core_now, 1 - core_now]
    hops = sorted(
        (-(2 * min(dz, 4 - dz) + min(dx, 4 - dx)), -dc, dz, dx)
        for dz in range(4)
        for dx in range(4)
        for dc in range(2)
        if dz or dx or dc
    )
    return [z[dz] + x[dx] + core[-dc] for _, dc, dz, dx in hops]


def transform_tables(block_count, span_rows, own_channels):
    blocks = np.arange(block_count)
    times = np.arange(span_rows)
    across = 2.0 * math.pi * np.outer(2 * blocks + 1, blocks) / (4 * block_count)
    turn = 2.0 * math.pi * np.outer(2 * blocks + 1, times) / (4 * block_count * span_rows)
    within = 2.0 * math.pi * (np.outer(times, times) % span_rows) / span_rows
    each = np.eye(own_channels)
    across_fwd = np.concatenate([np.kron(np.cos(across), each), np.kron(-np.sin(across), each)], axis=0)
    across_inv = across_fwd.T / (block_count * span_rows)
    within_fwd = np.block([[np.cos(within), -np.sin(within)], [np.sin(within), np.cos(within)]])
    turn_cos = np.repeat(np.cos(turn), own_channels, axis=0)
    turn_sin = np.repeat(np.sin(turn), own_channels, axis=0)
    return (
        jnp.asarray(across_fwd, BF16),
        jnp.asarray(across_inv, BF16),
        jnp.asarray(within_fwd, BF16),
        jnp.asarray(within_fwd.T, BF16),
        jnp.asarray(turn_cos, F32),
        jnp.asarray(turn_sin, F32),
    )


def layer_kernel(
    n_seq,
    n_ch,
    q_hbm,
    k_hbm,
    v_hbm,
    h_hbm,
    og_hbm,
    w_hbm,
    kf_hbm,
    ki_hbm,
    df_hbm,
    di_hbm,
    tc_hbm,
    ts_hbm,
    mixed_ref,
    qg_ref,
    dd,
    q_ref,
    k_ref,
    v_ref,
    h_ref,
    og_ref,
    w,
    kf,
    ki,
    df,
    di,
    tc,
    ts,
    uh_src,
    uh,
    cv_src,
    cv,
    g_src,
    g,
    dd_src,
    og,
    rs_src,
    rs,
    level,
    spec_uh,
    spec_out,
    turned,
    gg,
    load_sem,
    send_sem,
    recv_sem,
    ag_send,
    ag_recv,
    rs_send,
    rs_recv,
):
    seq = lax.axis_index("seq")
    ch = lax.axis_index("ch")
    rows, width = q_hbm.shape
    lanes = rows
    half = n_seq * (width // n_seq)
    part = width
    step_rows = min(128, half)
    n_y = n_ch // 2
    plane, row = ch // n_y, ch % n_y

    def column(d_plane, d_row):
        return ((plane + d_plane) % 2) * n_y + (row + d_row) % n_y

    far_first = peers_far_first(seq, n_seq)

    loads = [
        pltpu.make_async_copy(src, dst, load_sem.at[i])
        for i, (src, dst) in enumerate(
            [
                (k_hbm, k_ref),
                (v_hbm, v_ref),
                (h_hbm, h_ref),
                (og_hbm, og_ref),
                (kf_hbm, kf),
                (tc_hbm, tc),
                (ts_hbm, ts),
                (df_hbm, df),
                (di_hbm, di),
                (ki_hbm, ki),
                (w_hbm, w),
                (q_hbm, q_ref),
            ]
        )
    ]
    for load in loads:
        load.start()

    barrier = pltpu.get_barrier_semaphore()

    with jax.named_scope("greet"):
        for peer in far_first:
            pl.semaphore_signal(barrier, inc=1, device_id={"seq": peer}, device_id_type=MESH)
        for d_plane, d_row in GREETED:
            pl.semaphore_signal(
                barrier, inc=1, device_id={"ch": column(d_plane, d_row)}, device_id_type=MESH
            )

    with jax.named_scope("product"):
        for load in loads[:3]:
            load.wait()
        u = (k_ref[...].astype(F32) * v_ref[...].astype(F32)).astype(BF16)
        uh_src[:, :, :lanes] = u.T.reshape(n_seq, width // n_seq, rows)
        uh_src[:, :, lanes:] = h_ref[...].T.reshape(n_seq, width // n_seq, rows)

    with jax.named_scope("barrier"):
        pl.semaphore_wait(barrier, n_seq - 1 + len(GREETED))

    def exchange(src, dst, slot):
        for peer in far_first:
            pltpu.make_async_remote_copy(
                src_ref=src.at[peer],
                dst_ref=dst.at[seq],
                send_sem=send_sem.at[slot],
                recv_sem=recv_sem.at[slot],
                device_id={"seq": peer},
                device_id_type=MESH,
            ).start()
        dst[seq] = src[seq]

    def arrived(dst, slot):
        landed = dst.at[pl.ds(0, n_seq - 1)]
        pltpu.make_async_copy(landed, landed, recv_sem.at[slot]).wait()

    def departed(src, slot):
        left = src.at[pl.ds(0, n_seq - 1)]
        pltpu.make_async_copy(left, left, send_sem.at[slot]).wait()

    def gather_copy(kind):
        moved = GATHER_BLOCKS[kind]
        block = column(*moved)
        return pltpu.make_async_remote_copy(
            src_ref=og_ref if moved == (0, 0) else og.at[block],
            dst_ref=og.at[block],
            send_sem=ag_send.at[kind],
            recv_sem=ag_recv.at[kind],
            device_id={"ch": column(*GATHER_ROUTES[kind])},
            device_id_type=MESH,
        )

    with jax.named_scope("send_uh_og"):
        exchange(uh_src, uh, 0)
        loads[3].wait()
        for kind in range(4):
            gather_copy(kind).start()
        for load in loads[4:10]:
            load.wait()
    with jax.named_scope("pass_on_og"):
        for needed, kinds in GATHER_PASSED:
            gather_copy(needed).wait_recv()
            for kind in kinds:
                gather_copy(kind).start()

    def forward(values, count, put):
        level[:, : count * lanes] = jnp.dot(kf[...], values, preferred_element_type=F32)
        for r in range(0, half, step_rows):
            c, s = tc[r : r + step_rows, :], ts[r : r + step_rows, :]
            for a in range(count):
                re = level[r : r + step_rows, a * lanes : (a + 1) * lanes]
                im = level[half + r : half + r + step_rows, a * lanes : (a + 1) * lanes]
                z = jnp.concatenate([re * c + im * s, im * c - re * s], axis=1).astype(BF16)
                put(r, a, jnp.dot(z, df[...], preferred_element_type=F32))

    def inverse(product, count, dst):
        for r in range(0, half, step_rows):
            c, s = tc[r : r + step_rows, :], ts[r : r + step_rows, :]
            for a in range(count):
                x = jnp.dot(product(r, a), di[...], preferred_element_type=F32)
                re, im = x[:, :lanes], x[:, lanes:]
                turned[r : r + step_rows, a * lanes : (a + 1) * lanes] = (re * c - im * s).astype(BF16)
                turned[half + r : half + r + step_rows, a * lanes : (a + 1) * lanes] = (
                    im * c + re * s
                ).astype(BF16)
        y = jnp.dot(ki[...], turned[:, : count * lanes], preferred_element_type=F32)
        dst[...] = y.astype(BF16).reshape(dst.shape)

    def put_uh(r, a, value):
        spec_uh[a, r : r + step_rows, :] = value

    def conv_product(r, a):
        x, y = spec_uh[0, r : r + step_rows, :], spec_uh[1, r : r + step_rows, :]
        xr, xi, yr, yi = x[:, :lanes], x[:, lanes:], y[:, :lanes], y[:, lanes:]
        return jnp.concatenate([xr * yr - xi * yi, xr * yi + xi * yr], axis=1).astype(BF16)

    with jax.named_scope("wait_uh"):
        arrived(uh, 0)
    with jax.named_scope("forward_uh"):
        forward(uh[...].reshape(half, 2 * lanes), 2, put_uh)
    with jax.named_scope("inverse_conv"):
        inverse(conv_product, 1, cv_src)
    with jax.named_scope("send_conv"):
        exchange(cv_src, cv, 1)

    loads[10].wait()
    loads[11].wait()

    def grad_block(value, source):
        columns = pl.ds(pl.multiple_of(source * part, part), part)
        return lax.dot_general(value, w[:, columns], (((1,), (1,)), ((), ())), preferred_element_type=F32)

    with jax.named_scope("gate_grad"):
        gg[...] = grad_block(og_ref[...], ch)
        for kind in GATHER_ORDER:
            if kind >= len(GATHER_PASSED):
                gather_copy(kind).wait_recv()
            source = column(*GATHER_SOURCES[kind])
            gg[...] += grad_block(og[source], source)
    with jax.named_scope("send_g"):
        conv_grad = (gg[...] * q_ref[...].astype(F32)).astype(BF16)
        g_src[...] = conv_grad.T.reshape(g_src.shape)
        exchange(g_src, g, 2)

    with jax.named_scope("wait_conv"):
        arrived(cv, 1)
    with jax.named_scope("gate"):
        conv = cv[...].reshape(width, rows).T.astype(F32)
        qg_ref[...] = (gg[...] * conv).astype(BF16)
        gated = (q_ref[...].astype(F32) * conv).astype(BF16)

    def scatter_copy(kind):
        return pltpu.make_async_remote_copy(
            src_ref=rs_src.at[kind],
            dst_ref=rs.at[kind],
            send_sem=rs_send.at[kind],
            recv_sem=rs_recv.at[kind],
            device_id={"ch": column(*SCATTER_ROUTES[kind])},
            device_id_type=MESH,
        )

    def out_block(target):
        columns = pl.ds(pl.multiple_of(target * part, part), part)
        return jnp.dot(gated, w[:, columns], preferred_element_type=F32)

    def send_block(kind):
        total = out_block(column(*SCATTER_BLOCKS[kind]))
        for earlier in SCATTER_ADDS[kind]:
            scatter_copy(earlier).wait_recv()
            total = total + rs[earlier].astype(F32)
        rs_src[kind] = total.astype(BF16)
        scatter_copy(kind).start()

    with jax.named_scope("out_blocks"):
        for kind in range(5):
            send_block(kind)

    def put_g(r, a, value):
        gr, gi = value[:, :lanes], value[:, lanes:]
        for b in range(2):
            x = spec_uh[1 - b, r : r + step_rows, :]
            xr, xi = x[:, :lanes], x[:, lanes:]
            spec_out[b, r : r + step_rows, :] = jnp.concatenate(
                [xr * gr + xi * gi, xr * gi - xi * gr], axis=1
            ).astype(BF16)

    with jax.named_scope("wait_g"):
        arrived(g, 2)
    with jax.named_scope("forward_g"):
        forward(g[...].reshape(half, lanes), 1, put_g)
    with jax.named_scope("inverse_grads"):
        inverse(lambda r, a: spec_out[a, r : r + step_rows, :], 2, dd_src)
    with jax.named_scope("send_grads"):
        exchange(dd_src, dd, 3)

    with jax.named_scope("mixed_sum"):
        send_block(5)
        send_block(6)
        total = out_block(ch)
        for kind in range(3, 7):
            scatter_copy(kind).wait_recv()
            total = total + rs[kind].astype(F32)
        mixed_ref[...] = total.astype(BF16)

    with jax.named_scope("wait_grads"):
        arrived(dd, 3)
    with jax.named_scope("departures"):
        departed(uh_src, 0)
        departed(cv_src, 1)
        departed(g_src, 2)
        departed(dd_src, 3)
        for kind in range(7):
            gather_copy(kind).wait_send()
            scatter_copy(kind).wait_send()


def finish_kernel(
    mixed_in, qg_in, dd, k_hbm, v_hbm, mixed_out, qg_out, kg_out, vg_out, fg_out, k_ref, v_ref, kg, vg, fg, sem
):
    n_seq, own, lanes = dd.shape
    rows, width = k_ref.shape
    lanes = lanes // 2
    first = [
        pltpu.make_async_copy(src, dst, sem.at[i])
        for i, (src, dst) in enumerate([(k_hbm, k_ref), (v_hbm, v_ref), (mixed_in, mixed_out), (qg_in, qg_out)])
    ]
    last = [
        pltpu.make_async_copy(src, dst, sem.at[4 + i])
        for i, (src, dst) in enumerate([(fg, fg_out), (kg, kg_out), (vg, vg_out)])
    ]
    for copy in first:
        copy.start()
    fg[...] = dd[:, :, lanes:].reshape(width, rows).T.astype(F32)
    last[0].start()
    u_grad = dd[:, :, :lanes].reshape(width, rows).T.astype(F32)
    first[0].wait()
    first[1].wait()
    kg[...] = (u_grad * v_ref[...].astype(F32)).astype(BF16)
    last[1].start()
    vg[...] = (u_grad * k_ref[...].astype(F32)).astype(BF16)
    last[2].start()
    for copy in first[2:] + last:
        copy.wait()


def per_device(query_act, key_act, value_act, filter_taps, out_grad, out_weight):
    rows, width = query_act.shape
    n_seq, n_ch = lax.axis_size("seq"), lax.axis_size("ch")
    own = width // n_seq
    tables = transform_tables(n_seq, rows, own)
    half = n_seq * own
    vmem, anywhere = pl.BlockSpec(memory_space=pltpu.VMEM), pl.BlockSpec(memory_space=pl.ANY)
    bf = jax.ShapeDtypeStruct((rows, width), BF16)

    def blocks(lanes):
        return pltpu.VMEM((n_seq, own, lanes), BF16)

    full = pltpu.VMEM((rows, width), BF16)
    mixed, query_grad, sums = pl.pallas_call(
        functools.partial(layer_kernel, n_seq, n_ch),
        out_shape=(bf, bf, jax.ShapeDtypeStruct((n_seq, own, 2 * rows), BF16)),
        in_specs=[anywhere] * 12,
        out_specs=(vmem,) * 3,
        scratch_shapes=[
            full,
            full,
            full,
            full,
            full,
            pltpu.VMEM(out_weight.shape, BF16),
            *[pltpu.VMEM(t.shape, t.dtype) for t in tables],
            blocks(2 * rows),
            blocks(2 * rows),
            blocks(rows),
            blocks(rows),
            blocks(rows),
            blocks(rows),
            blocks(2 * rows),
            pltpu.VMEM((n_ch, rows, width), BF16),
            pltpu.VMEM((7, rows, width), BF16),
            pltpu.VMEM((7, rows, width), BF16),
            pltpu.VMEM((2 * half, 2 * rows), F32),
            pltpu.VMEM((2, half, 2 * rows), F32),
            pltpu.VMEM((2, half, 2 * rows), BF16),
            pltpu.VMEM((2 * half, 2 * rows), BF16),
            pltpu.VMEM((rows, width), F32),
            pltpu.SemaphoreType.DMA((12,)),
            pltpu.SemaphoreType.DMA((4,)),
            pltpu.SemaphoreType.DMA((4,)),
            pltpu.SemaphoreType.DMA((7,)),
            pltpu.SemaphoreType.DMA((7,)),
            pltpu.SemaphoreType.DMA((7,)),
            pltpu.SemaphoreType.DMA((7,)),
        ],
        compiler_params=pltpu.CompilerParams(
            collective_id=0, has_side_effects=True, vmem_limit_bytes=60 * 1024 * 1024
        ),
    )(query_act, key_act, value_act, filter_taps, out_grad, out_weight, *tables)
    return pl.pallas_call(
        finish_kernel,
        out_shape=(bf, bf, bf, bf, jax.ShapeDtypeStruct((rows, width), F32)),
        in_specs=[vmem, vmem, vmem, anywhere, anywhere],
        out_specs=(anywhere,) * 5,
        scratch_shapes=[full] * 4 + [pltpu.VMEM((rows, width), F32), pltpu.SemaphoreType.DMA((7,))],
        compiler_params=pltpu.CompilerParams(vmem_limit_bytes=60 * 1024 * 1024),
    )(mixed, query_grad, sums, key_act, value_act)


def solution(mesh):
    return jax.shard_map(
        per_device,
        mesh=mesh,
        in_specs=(P("seq", "ch"),) * 5 + (P("ch", None),),
        out_specs=(P("seq", "ch"),) * 5,
        check_vma=False,
    )
```

time: 74.9 us -> 50.6 us (0.68)
  the two profiles are of different devices: /device:TPU:25 before, /device:TPU:1 now
where the time goes in v2:
time: 50.6 us; the launch traced here: 50.4 us
  Pallas kernels  49.8 us (98%)
  between operations  0.64 us (1%)
    pallas_call x1, Pallas kernels, per_device(): pl.pallas_call(functools.partial(layer_kernel, n_seq, n_ch), out_shape=(b...  46.8 us
    pallas_call x1, Pallas kernels, per_device(): pl.pallas_call(finish_kernel, out_shape=(bf, bf, bf, bf, jax.ShapeDtypeSt...  3.04 us

profile of v2, /device:TPU:1, one launch (start us, length us, event | category | flops | bytes accessed | tf_op | source)
XLA Modules:
  0.0 50.4 jit_solution(3834808902683697206)
XLA Ops:
  0.6 46.8 %shard_map.155 = (bf16[128,512]{1,0:T(8,128)(2,1)}, bf16[128,512]{1,0:T(8,128)(2,1)}, bf16[32,16,256]{2,1,0:T(8,128)(2,1)}) custom-call(bf16[128,512]{1,0:T(8,128)(2,1)} %q_hbm.1, bf16[128,512]{1,0:T(8,128)(2,1)} %k_hbm.3, bf16[128,512]{1,0:T(8,128)(2,1)} %v_hbm.3, bf16[128,512]{1,0:T(8,128)(2,1)} %h_hbm.1, bf16[128,512]{1,0:T(8,128)(2,1)} %og_hbm.1, ...), custom_call_target="tpu_custom_call" | custom-call | tf_op jit(solution)/shard_map/pallas_call | solution.py:396
  47.4 3.0 %shard_map.156 = (bf16[128,512]{1,0:T(8,128)(2,1)}, bf16[128,512]{1,0:T(8,128)(2,1)}, bf16[128,512]{1,0:T(8,128)(2,1)}, bf16[128,512]{1,0:T(8,128)(2,1)}, f32[128,512]{1,0:T(8,128)}) custom-call(bf16[128,512]{1,0:T(8,128)(2,1)} %get-tuple-element.8.mixed_in, bf16[128,512]{1,0:T(8,128)(2,1)} %get-tuple-element.9.qg_in, ...), custom_call_target="tpu_custom_call" | custom-call | tf_op jit(solution)/shard_map/pallas_call | solution.py:436

commit v3 on v2

--- a/solution.py
+++ b/solution.py
@@ -17,8 +17,9 @@
 NEAR = ((0, 1), (0, -1))
 GATHER_ROUTES = ((1, 0), (0, 2)) + NEAR + NEAR + ((1, 0),)
 GATHER_BLOCKS = ((0, 0),) * 4 + ((1, 0), (1, 0), (0, 2))
-GATHER_PASSED = ((0, (4, 5)), (1, (6,)))
+GATHER_PASSED = {0: (4, 5), 1: (6,)}
 GATHER_SOURCES = ((1, 0), (0, 2), (0, -1), (0, 1), (1, -1), (1, 1), (1, 2))
+EARLY = 2
 GATHER_ORDER = (0, 1, 2, 3, 4, 5, 6)
 SCATTER_ROUTES = ((1, 0),) + NEAR + NEAR + ((0, 2), (1, 0))
 SCATTER_BLOCKS = ((1, 2), (1, 1), (1, -1), (0, 1), (0, -1), (0, 2), (1, 0))
@@ -172,6 +173,15 @@
         uh_src[:, :, :lanes] = u.T.reshape(n_seq, width // n_seq, rows)
         uh_src[:, :, lanes:] = h_ref[...].T.reshape(n_seq, width // n_seq, rows)
 
+    def grad_block(value, source):
+        columns = pl.ds(pl.multiple_of(source * part, part), part)
+        return lax.dot_general(value, w[:, columns], (((1,), (1,)), ((), ())), preferred_element_type=F32)
+
+    with jax.named_scope("own_gate_grad"):
+        loads[3].wait()
+        loads[10].wait()
+        gg[...] = grad_block(og_ref[...], ch)
+
     with jax.named_scope("barrier"):
         pl.semaphore_wait(barrier, n_seq - 1 + len(GREETED))
 
@@ -208,17 +218,24 @@
         )
 
     with jax.named_scope("send_uh_og"):
-        exchange(uh_src, uh, 0)
-        loads[3].wait()
         for kind in range(4):
             gather_copy(kind).start()
+        exchange(uh_src, uh, 0)
         for load in loads[4:10]:
             load.wait()
-    with jax.named_scope("pass_on_og"):
-        for needed, kinds in GATHER_PASSED:
-            gather_copy(needed).wait_recv()
-            for kind in kinds:
-                gather_copy(kind).start()
+    def add_grad_block(kind):
+        source = column(*GATHER_SOURCES[kind])
+        gg[...] += grad_block(og[source], source)
+
+    def collect(kinds):
+        for kind in kinds:
+            gather_copy(kind).wait_recv()
+            for passed in GATHER_PASSED.get(kind, ()):
+                gather_copy(passed).start()
+            add_grad_block(kind)
+
+    with jax.named_scope("gate_grad_early"):
+        collect(GATHER_ORDER[:EARLY])
 
     def forward(values, count, put):
         level[:, : count * lanes] = jnp.dot(kf[...], values, preferred_element_type=F32)
@@ -260,20 +277,10 @@
     with jax.named_scope("send_conv"):
         exchange(cv_src, cv, 1)
 
-    loads[10].wait()
-    loads[11].wait()
-
-    def grad_block(value, source):
-        columns = pl.ds(pl.multiple_of(source * part, part), part)
-        return lax.dot_general(value, w[:, columns], (((1,), (1,)), ((), ())), preferred_element_type=F32)
-
-    with jax.named_scope("gate_grad"):
-        gg[...] = grad_block(og_ref[...], ch)
-        for kind in GATHER_ORDER:
-            if kind >= len(GATHER_PASSED):
-                gather_copy(kind).wait_recv()
-            source = column(*GATHER_SOURCES[kind])
-            gg[...] += grad_block(og[source], source)
+    with jax.named_scope("gate_grad_late"):
+        collect(GATHER_ORDER[EARLY:])
+        loads[11].wait()
+
     with jax.named_scope("send_g"):
         conv_grad = (gg[...] * q_ref[...].astype(F32)).astype(BF16)
         g_src[...] = conv_grad.T.reshape(g_src.shape)
@@ -386,17 +393,18 @@
     own = width // n_seq
     tables = transform_tables(n_seq, rows, own)
     half = n_seq * own
-    vmem, anywhere = pl.BlockSpec(memory_space=pltpu.VMEM), pl.BlockSpec(memory_space=pl.ANY)
+    vmem, fixed = pl.BlockSpec(memory_space=pltpu.VMEM), pl.BlockSpec(memory_space=pltpu.HBM)
     bf = jax.ShapeDtypeStruct((rows, width), BF16)
 
     def blocks(lanes):
         return pltpu.VMEM((n_seq, own, lanes), BF16)
 
     full = pltpu.VMEM((rows, width), BF16)
+    operands = (query_act, key_act, value_act, filter_taps, out_grad, out_weight, *tables)
     mixed, query_grad, sums = pl.pallas_call(
         functools.partial(layer_kernel, n_seq, n_ch),
         out_shape=(bf, bf, jax.ShapeDtypeStruct((n_seq, own, 2 * rows), BF16)),
-        in_specs=[anywhere] * 12,
+        in_specs=[fixed] * 12,
         out_specs=(vmem,) * 3,
         scratch_shapes=[
             full,
@@ -430,16 +438,16 @@
             pltpu.SemaphoreType.DMA((7,)),
         ],
         compiler_params=pltpu.CompilerParams(
-            collective_id=0, has_side_effects=True, vmem_limit_bytes=60 * 1024 * 1024
+            collective_id=0, has_side_effects=True, vmem_limit_bytes=32 * 1024 * 1024
         ),
-    )(query_act, key_act, value_act, filter_taps, out_grad, out_weight, *tables)
+    )(*[pltpu.with_memory_space_constraint(a, pltpu.HBM) for a in operands])
     return pl.pallas_call(
         finish_kernel,
         out_shape=(bf, bf, bf, bf, jax.ShapeDtypeStruct((rows, width), F32)),
-        in_specs=[vmem, vmem, vmem, anywhere, anywhere],
-        out_specs=(anywhere,) * 5,
+        in_specs=[vmem, vmem, vmem, fixed, fixed],
+        out_specs=(fixed,) * 5,
         scratch_shapes=[full] * 4 + [pltpu.VMEM((rows, width), F32), pltpu.SemaphoreType.DMA((7,))],
-        compiler_params=pltpu.CompilerParams(vmem_limit_bytes=60 * 1024 * 1024),
+        compiler_params=pltpu.CompilerParams(vmem_limit_bytes=32 * 1024 * 1024),
     )(mixed, query_grad, sums, key_act, value_act)
 
 

time: 50.6 us -> 47.4 us (0.937)
  Pallas kernels: 49.8 us -> 46.7 us
    pallas_call x1, Pallas kernels: 3.04 us -> 1.3 us  [per_device(): pl.pallas_call(finish_kernel, out_shape=(bf, bf, bf, bf, jax.ShapeDtypeSt...]
    pallas_call x1, Pallas kernels: 46.8 us -> 45.4 us  [per_device(): pl.pallas_call(functools.partial(layer_kernel, n_seq, n_ch), out_shape=(b...]
where the time goes in v3:
time: 47.4 us; the launch traced here: 47.3 us
  Pallas kernels  46.7 us (99%)
  between operations  0.67 us (1%)
    pallas_call x1, Pallas kernels, per_device(): pl.pallas_call(functools.partial(layer_kernel, n_seq, n_ch), out_shape=(b...  45.4 us
    pallas_call x1, Pallas kernels, per_device(): pl.pallas_call(finish_kernel, out_shape=(bf, bf, bf, bf, jax.ShapeDtypeSt...  1.3 us

profile of v3, /device:TPU:1, one launch (start us, length us, event | category | flops | bytes accessed | tf_op | source)
XLA Modules:
  0.0 47.3 jit_solution(16441300824570469634)
XLA Ops:
  0.6 0.0 copy-start.1
  0.6 0.0 copy-start
  0.7 45.4 %shard_map.155 = (bf16[128,512]{1,0:T(8,128)(2,1)S(1)}, bf16[128,512]{1,0:T(8,128)(2,1)S(1)}, bf16[32,16,256]{2,1,0:T(8,128)(2,1)S(1)}) custom-call(bf16[128,512]{1,0:T(8,128)(2,1)} %q_hbm.1, bf16[128,512]{1,0:T(8,128)(2,1)} %k_hbm.3, bf16[128,512]{1,0:T(8,128)(2,1)} %v_hbm.3, bf16[128,512]{1,0:T(8,128)(2,1)} %h_hbm.1, bf16[128,512]{1,0:T(8,128)(2,1)} %og_hbm.1, ...), custom_call_target="tpu_custom_call" | custom-call | tf_op jit(solution)/shard_map/pallas_call | solution.py:404
  46.0 0.0 copy-done.1
  46.0 0.0 copy-done
  46.0 1.3 %shard_map.156 = (bf16[128,512]{1,0:T(8,128)(2,1)}, bf16[128,512]{1,0:T(8,128)(2,1)}, bf16[128,512]{1,0:T(8,128)(2,1)}, bf16[128,512]{1,0:T(8,128)(2,1)}, f32[128,512]{1,0:T(8,128)}) custom-call(bf16[128,512]{1,0:T(8,128)(2,1)S(1)} %get-tuple-element.8.mixed_in, bf16[128,512]{1,0:T(8,128)(2,1)S(1)} %get-tuple-element.9.qg_in, ...), custom_call_target="tpu_custom_call" | custom-call | tf_op jit(solution)/shard_map/pallas_call | solution.py:444
Async XLA Ops:
  0.6 45.4 %copy-start.1 = (bf16[128,512]{1,0:T(8,128)(2,1)S(1)}, bf16[128,512]{1,0:T(8,128)(2,1)}, u32[]{:S(2)}) copy-start(bf16[128,512]{1,0:T(8,128)(2,1)} %v_hbm.3) | copy-start | bytes 393220
  0.6 45.4 %copy-start = (bf16[128,512]{1,0:T(8,128)(2,1)S(1)}, bf16[128,512]{1,0:T(8,128)(2,1)}, u32[]{:S(2)}) copy-start(bf16[128,512]{1,0:T(8,128)(2,1)} %k_hbm.3) | copy-start | bytes 393220

commit v4 on v3

--- a/solution.py
+++ b/solution.py
@@ -14,17 +14,36 @@
 BF16 = jnp.bfloat16
 
 
-NEAR = ((0, 1), (0, -1))
-GATHER_ROUTES = ((1, 0), (0, 2)) + NEAR + NEAR + ((1, 0),)
-GATHER_BLOCKS = ((0, 0),) * 4 + ((1, 0), (1, 0), (0, 2))
-GATHER_PASSED = {0: (4, 5), 1: (6,)}
-GATHER_SOURCES = ((1, 0), (0, 2), (0, -1), (0, 1), (1, -1), (1, 1), (1, 2))
-EARLY = 2
-GATHER_ORDER = (0, 1, 2, 3, 4, 5, 6)
-SCATTER_ROUTES = ((1, 0),) + NEAR + NEAR + ((0, 2), (1, 0))
-SCATTER_BLOCKS = ((1, 2), (1, 1), (1, -1), (0, 1), (0, -1), (0, 2), (1, 0))
-SCATTER_ADDS = ((), (), (), (), (), (0,), (1, 2))
-GREETED = ((1, 0), (0, 2)) + NEAR
+ALL, FIRST, SECOND = 0, 1, 2
+UP, DOWN, ACROSS, FAR = (0, 1), (0, -1), (1, 0), (0, 2)
+OWN = (0, 0)
+GATHER_MOVES = (
+    (OWN, ALL, ACROSS),
+    (OWN, FIRST, FAR),
+    (OWN, SECOND, FAR),
+    (OWN, ALL, UP),
+    (OWN, ALL, DOWN),
+    (ACROSS, ALL, UP),
+    (ACROSS, ALL, DOWN),
+    (FAR, FIRST, ACROSS),
+    (FAR, SECOND, ACROSS),
+)
+GATHER_PASSED = {0: (5, 6), 1: (7,), 2: (8,)}
+GATHER_SOURCES = {0: ACROSS, 2: FAR, 3: DOWN, 4: UP, 5: (1, -1), 6: (1, 1), 8: (1, 2)}
+EARLY = 5
+SCATTER_MOVES = (
+    ((1, 2), ALL, ACROSS),
+    ((1, 1), ALL, UP),
+    ((1, -1), ALL, DOWN),
+    (UP, ALL, UP),
+    (DOWN, ALL, DOWN),
+    (FAR, ALL, FAR),
+    (ACROSS, ALL, ACROSS),
+)
+SCATTER_ADDS = {5: (0,), 6: (1, 2)}
+BEFORE = 5
+SCATTER_LAST = (3, 4, 5, 6)
+GREETED = (ACROSS, FAR, UP, DOWN)
 
 
 def peers_far_first(seq, n_seq):
@@ -83,7 +102,8 @@
     ts_hbm,
     mixed_ref,
     qg_ref,
-    dd,
+    du,
+    dh,
     q_ref,
     k_ref,
     v_ref,
@@ -102,7 +122,8 @@
     cv,
     g_src,
     g,
-    dd_src,
+    du_src,
+    dh_src,
     og,
     rs_src,
     rs,
@@ -111,6 +132,7 @@
     spec_out,
     turned,
     gg,
+    q_turned,
     load_sem,
     send_sem,
     recv_sem,
@@ -133,6 +155,17 @@
         return ((plane + d_plane) % 2) * n_y + (row + d_row) % n_y
 
     far_first = peers_far_first(seq, n_seq)
+    some_rows = (pl.ds(0, rows), pl.ds(0, rows // 2), pl.ds(rows // 2, rows // 2))
+
+    barrier = pltpu.get_barrier_semaphore()
+
+    with jax.named_scope("greet"):
+        for peer in far_first:
+            pl.semaphore_signal(barrier, inc=1, device_id={"seq": peer}, device_id_type=MESH)
+        for d_plane, d_row in GREETED:
+            pl.semaphore_signal(
+                barrier, inc=1, device_id={"ch": column(d_plane, d_row)}, device_id_type=MESH
+            )
 
     loads = [
         pltpu.make_async_copy(src, dst, load_sem.at[i])
@@ -156,16 +189,6 @@
     for load in loads:
         load.start()
 
-    barrier = pltpu.get_barrier_semaphore()
-
-    with jax.named_scope("greet"):
-        for peer in far_first:
-            pl.semaphore_signal(barrier, inc=1, device_id={"seq": peer}, device_id_type=MESH)
-        for d_plane, d_row in GREETED:
-            pl.semaphore_signal(
-                barrier, inc=1, device_id={"ch": column(d_plane, d_row)}, device_id_type=MESH
-            )
-
     with jax.named_scope("product"):
         for load in loads[:3]:
             load.wait()
@@ -175,9 +198,11 @@
 
     def grad_block(value, source):
         columns = pl.ds(pl.multiple_of(source * part, part), part)
-        return lax.dot_general(value, w[:, columns], (((1,), (1,)), ((), ())), preferred_element_type=F32)
+        return lax.dot_general(w[:, columns], value, (((1,), (1,)), ((), ())), preferred_element_type=F32)
 
     with jax.named_scope("own_gate_grad"):
+        loads[11].wait()
+        q_turned[...] = q_ref[...].T
         loads[3].wait()
         loads[10].wait()
         gg[...] = grad_block(og_ref[...], ch)
@@ -206,19 +231,19 @@
         pltpu.make_async_copy(left, left, send_sem.at[slot]).wait()
 
     def gather_copy(kind):
-        moved = GATHER_BLOCKS[kind]
-        block = column(*moved)
+        moved, extent, goal = GATHER_MOVES[kind]
+        block, extent = column(*moved), some_rows[extent]
         return pltpu.make_async_remote_copy(
-            src_ref=og_ref if moved == (0, 0) else og.at[block],
-            dst_ref=og.at[block],
+            src_ref=og_ref.at[extent] if moved == OWN else og.at[block, extent],
+            dst_ref=og.at[block, extent],
             send_sem=ag_send.at[kind],
             recv_sem=ag_recv.at[kind],
-            device_id={"ch": column(*GATHER_ROUTES[kind])},
+            device_id={"ch": column(*goal)},
             device_id_type=MESH,
         )
 
     with jax.named_scope("send_uh_og"):
-        for kind in range(4):
+        for kind in [i for i, move in enumerate(GATHER_MOVES) if move[0] == OWN]:
             gather_copy(kind).start()
         exchange(uh_src, uh, 0)
         for load in loads[4:10]:
@@ -232,10 +257,11 @@
             gather_copy(kind).wait_recv()
             for passed in GATHER_PASSED.get(kind, ()):
                 gather_copy(passed).start()
-            add_grad_block(kind)
+            if kind in GATHER_SOURCES:
+                add_grad_block(kind)
 
     with jax.named_scope("gate_grad_early"):
-        collect(GATHER_ORDER[:EARLY])
+        collect(range(EARLY))
 
     def forward(values, count, put):
         level[:, : count * lanes] = jnp.dot(kf[...], values, preferred_element_type=F32)
@@ -278,28 +304,28 @@
         exchange(cv_src, cv, 1)
 
     with jax.named_scope("gate_grad_late"):
-        collect(GATHER_ORDER[EARLY:])
-        loads[11].wait()
+        collect(range(EARLY, len(GATHER_MOVES)))
 
     with jax.named_scope("send_g"):
-        conv_grad = (gg[...] * q_ref[...].astype(F32)).astype(BF16)
-        g_src[...] = conv_grad.T.reshape(g_src.shape)
+        conv_grad = (gg[...] * q_turned[...].astype(F32)).astype(BF16)
+        g_src[...] = conv_grad.reshape(g_src.shape)
         exchange(g_src, g, 2)
 
     with jax.named_scope("wait_conv"):
         arrived(cv, 1)
     with jax.named_scope("gate"):
         conv = cv[...].reshape(width, rows).T.astype(F32)
-        qg_ref[...] = (gg[...] * conv).astype(BF16)
         gated = (q_ref[...].astype(F32) * conv).astype(BF16)
 
     def scatter_copy(kind):
+        _, extent, goal = SCATTER_MOVES[kind]
+        extent = some_rows[extent]
         return pltpu.make_async_remote_copy(
-            src_ref=rs_src.at[kind],
-            dst_ref=rs.at[kind],
+            src_ref=rs_src.at[kind, extent],
+            dst_ref=rs.at[kind, extent],
             send_sem=rs_send.at[kind],
             recv_sem=rs_recv.at[kind],
-            device_id={"ch": column(*SCATTER_ROUTES[kind])},
+            device_id={"ch": column(*goal)},
             device_id_type=MESH,
         )
 
@@ -308,15 +334,15 @@
         return jnp.dot(gated, w[:, columns], preferred_element_type=F32)
 
     def send_block(kind):
-        total = out_block(column(*SCATTER_BLOCKS[kind]))
-        for earlier in SCATTER_ADDS[kind]:
+        total = out_block(column(*SCATTER_MOVES[kind][0]))
+        for earlier in SCATTER_ADDS.get(kind, ()):
             scatter_copy(earlier).wait_recv()
             total = total + rs[earlier].astype(F32)
         rs_src[kind] = total.astype(BF16)
         scatter_copy(kind).start()
 
     with jax.named_scope("out_blocks"):
-        for kind in range(5):
+        for kind in range(BEFORE):
             send_block(kind)
 
     def put_g(r, a, value):
@@ -332,38 +358,43 @@
         arrived(g, 2)
     with jax.named_scope("forward_g"):
         forward(g[...].reshape(half, lanes), 1, put_g)
-    with jax.named_scope("inverse_grads"):
-        inverse(lambda r, a: spec_out[a, r : r + step_rows, :], 2, dd_src)
-    with jax.named_scope("send_grads"):
-        exchange(dd_src, dd, 3)
+    for b, (src, dst) in enumerate(((du_src, du), (dh_src, dh))):
+        with jax.named_scope("inverse_grads"):
+            inverse(lambda r, a: spec_out[b, r : r + step_rows, :], 1, src)
+        with jax.named_scope("send_grads"):
+            exchange(src, dst, 3 + b)
 
     with jax.named_scope("mixed_sum"):
-        send_block(5)
-        send_block(6)
+        for kind in (6, 5):
+            send_block(kind)
+        with jax.named_scope("query_grad"):
+            query_grad = (gg[...] * cv[...].reshape(width, rows).astype(F32)).astype(BF16)
+            qg_ref[...] = query_grad.T
         total = out_block(ch)
-        for kind in range(3, 7):
+        for kind in SCATTER_LAST:
             scatter_copy(kind).wait_recv()
             total = total + rs[kind].astype(F32)
         mixed_ref[...] = total.astype(BF16)
 
     with jax.named_scope("wait_grads"):
-        arrived(dd, 3)
+        arrived(du, 3)
+        arrived(dh, 4)
     with jax.named_scope("departures"):
         departed(uh_src, 0)
         departed(cv_src, 1)
         departed(g_src, 2)
-        departed(dd_src, 3)
-        for kind in range(7):
+        departed(du_src, 3)
+        departed(dh_src, 4)
+        for kind in range(len(GATHER_MOVES)):
             gather_copy(kind).wait_send()
+        for kind in range(len(SCATTER_MOVES)):
             scatter_copy(kind).wait_send()
 
 
 def finish_kernel(
-    mixed_in, qg_in, dd, k_hbm, v_hbm, mixed_out, qg_out, kg_out, vg_out, fg_out, k_ref, v_ref, kg, vg, fg, sem
+    mixed_in, qg_in, du, dh, k_hbm, v_hbm, mixed_out, qg_out, kg_out, vg_out, fg_out, k_ref, v_ref, kg, vg, fg, sem
 ):
-    n_seq, own, lanes = dd.shape
     rows, width = k_ref.shape
-    lanes = lanes // 2
     first = [
         pltpu.make_async_copy(src, dst, sem.at[i])
         for i, (src, dst) in enumerate([(k_hbm, k_ref), (v_hbm, v_ref), (mixed_in, mixed_out), (qg_in, qg_out)])
@@ -374,9 +405,9 @@
     ]
     for copy in first:
         copy.start()
-    fg[...] = dd[:, :, lanes:].reshape(width, rows).T.astype(F32)
+    fg[...] = dh[...].reshape(width, rows).T.astype(F32)
     last[0].start()
-    u_grad = dd[:, :, :lanes].reshape(width, rows).T.astype(F32)
+    u_grad = du[...].reshape(width, rows).T.astype(F32)
     first[0].wait()
     first[1].wait()
     kg[...] = (u_grad * v_ref[...].astype(F32)).astype(BF16)
@@ -401,11 +432,11 @@
 
     full = pltpu.VMEM((rows, width), BF16)
     operands = (query_act, key_act, value_act, filter_taps, out_grad, out_weight, *tables)
-    mixed, query_grad, sums = pl.pallas_call(
+    mixed, query_grad, u_grad, filter_grad = pl.pallas_call(
         functools.partial(layer_kernel, n_seq, n_ch),
-        out_shape=(bf, bf, jax.ShapeDtypeStruct((n_seq, own, 2 * rows), BF16)),
+        out_shape=(bf, bf, *[jax.ShapeDtypeStruct((n_seq, own, rows), BF16)] * 2),
         in_specs=[fixed] * 12,
-        out_specs=(vmem,) * 3,
+        out_specs=(vmem,) * 4,
         scratch_shapes=[
             full,
             full,
@@ -420,22 +451,24 @@
             blocks(rows),
             blocks(rows),
             blocks(rows),
-            blocks(2 * rows),
+            blocks(rows),
+            blocks(rows),
             pltpu.VMEM((n_ch, rows, width), BF16),
-            pltpu.VMEM((7, rows, width), BF16),
-            pltpu.VMEM((7, rows, width), BF16),
+            pltpu.VMEM((len(SCATTER_MOVES), rows, width), BF16),
+            pltpu.VMEM((len(SCATTER_MOVES), rows, width), BF16),
             pltpu.VMEM((2 * half, 2 * rows), F32),
             pltpu.VMEM((2, half, 2 * rows), F32),
             pltpu.VMEM((2, half, 2 * rows), BF16),
             pltpu.VMEM((2 * half, 2 * rows), BF16),
-            pltpu.VMEM((rows, width), F32),
+            pltpu.VMEM((width, rows), F32),
+            pltpu.VMEM((width, rows), BF16),
             pltpu.SemaphoreType.DMA((12,)),
-            pltpu.SemaphoreType.DMA((4,)),
-            pltpu.SemaphoreType.DMA((4,)),
-            pltpu.SemaphoreType.DMA((7,)),
-            pltpu.SemaphoreType.DMA((7,)),
-            pltpu.SemaphoreType.DMA((7,)),
-            pltpu.SemaphoreType.DMA((7,)),
+            pltpu.SemaphoreType.DMA((5,)),
+            pltpu.SemaphoreType.DMA((5,)),
+            pltpu.SemaphoreType.DMA((len(GATHER_MOVES),)),
+            pltpu.SemaphoreType.DMA((len(GATHER_MOVES),)),
+            pltpu.SemaphoreType.DMA((len(SCATTER_MOVES),)),
+            pltpu.SemaphoreType.DMA((len(SCATTER_MOVES),)),
         ],
         compiler_params=pltpu.CompilerParams(
             collective_id=0, has_side_effects=True, vmem_limit_bytes=32 * 1024 * 1024
@@ -444,11 +477,11 @@
     return pl.pallas_call(
         finish_kernel,
         out_shape=(bf, bf, bf, bf, jax.ShapeDtypeStruct((rows, width), F32)),
-        in_specs=[vmem, vmem, vmem, fixed, fixed],
+        in_specs=[vmem, vmem, vmem, vmem, fixed, fixed],
         out_specs=(fixed,) * 5,
         scratch_shapes=[full] * 4 + [pltpu.VMEM((rows, width), F32), pltpu.SemaphoreType.DMA((7,))],
         compiler_params=pltpu.CompilerParams(vmem_limit_bytes=32 * 1024 * 1024),
-    )(mixed, query_grad, sums, key_act, value_act)
+    )(mixed, query_grad, u_grad, filter_grad, key_act, value_act)
 
 
 def solution(mesh):

time: 47.4 us -> 47.3 us (level)
  no operation moved by 1% of the time
where the time goes in v4:
time: 47.3 us; the launch traced here: 47.2 us
  Pallas kernels  46.5 us (98%)
  between operations  0.67 us (1%)
    pallas_call x1, Pallas kernels, per_device(): pl.pallas_call(functools.partial(layer_kernel, n_seq, n_ch), out_shape=(b...  45.2 us
    pallas_call x1, Pallas kernels, per_device(): pl.pallas_call(finish_kernel, out_shape=(bf, bf, bf, bf, jax.ShapeDtypeSt...  1.3 us

profile of v4, /device:TPU:1, one launch (start us, length us, event | category | flops | bytes accessed | tf_op | source)
XLA Modules:
  0.0 47.2 jit_solution(683739195496468650)
XLA Ops:
  0.6 0.0 copy-start.1
  0.6 0.0 copy-start
  0.7 45.2 %shard_map.155 = (bf16[128,512]{1,0:T(8,128)(2,1)S(1)}, bf16[128,512]{1,0:T(8,128)(2,1)S(1)}, bf16[32,16,128]{2,1,0:T(8,128)(2,1)S(1)}, bf16[32,16,128]{2,1,0:T(8,128)(2,1)S(1)}) custom-call(bf16[128,512]{1,0:T(8,128)(2,1)} %q_hbm.1, bf16[128,512]{1,0:T(8,128)(2,1)} %k_hbm.3, bf16[128,512]{1,0:T(8,128)(2,1)} %v_hbm.3, bf16[128,512]{1,0:T(8,128)(2,1)} %h_hbm.1, ...), custom_call_target="tpu_custom_call" | custom-call | tf_op jit(solution)/shard_map/pallas_call | solution.py:435
  45.9 0.0 copy-done.1
  45.9 0.0 copy-done
  45.9 1.3 %shard_map.156 = (bf16[128,512]{1,0:T(8,128)(2,1)}, bf16[128,512]{1,0:T(8,128)(2,1)}, bf16[128,512]{1,0:T(8,128)(2,1)}, bf16[128,512]{1,0:T(8,128)(2,1)}, f32[128,512]{1,0:T(8,128)}) custom-call(bf16[128,512]{1,0:T(8,128)(2,1)S(1)} %get-tuple-element.9.mixed_in, bf16[128,512]{1,0:T(8,128)(2,1)S(1)} %get-tuple-element.10.qg_in, ...), custom_call_target="tpu_custom_call" | custom-call | tf_op jit(solution)/shard_map/pallas_call | solution.py:477
Async XLA Ops:
  0.6 45.2 %copy-start.1 = (bf16[128,512]{1,0:T(8,128)(2,1)S(1)}, bf16[128,512]{1,0:T(8,128)(2,1)}, u32[]{:S(2)}) copy-start(bf16[128,512]{1,0:T(8,128)(2,1)} %v_hbm.3) | copy-start | bytes 393220
  0.6 45.2 %copy-start = (bf16[128,512]{1,0:T(8,128)(2,1)S(1)}, bf16[128,512]{1,0:T(8,128)(2,1)}, u32[]{:S(2)}) copy-start(bf16[128,512]{1,0:T(8,128)(2,1)} %k_hbm.3) | copy-start | bytes 393220

commit v5 on v4

--- a/solution.py
+++ b/solution.py
@@ -342,7 +342,7 @@
         scatter_copy(kind).start()
 
     with jax.named_scope("out_blocks"):
-        for kind in range(BEFORE):
+        for kind in (1, 2, 0, 3, 4):
             send_block(kind)
 
     def put_g(r, a, value):

time: 47.3 us -> 47.3 us (level)
  no operation moved by 1% of the time
where the time goes in v5:
time: 47.3 us; the launch traced here: 47.2 us
  Pallas kernels  46.5 us (98%)
  between operations  0.67 us (1%)
    pallas_call x1, Pallas kernels, per_device(): pl.pallas_call(functools.partial(layer_kernel, n_seq, n_ch), out_shape=(b...  45.2 us
    pallas_call x1, Pallas kernels, per_device(): pl.pallas_call(finish_kernel, out_shape=(bf, bf, bf, bf, jax.ShapeDtypeSt...  1.3 us

profile of v5, /device:TPU:1, one launch (start us, length us, event | category | flops | bytes accessed | tf_op | source)
XLA Modules:
  0.0 47.2 jit_solution(13217737804258082064)
XLA Ops:
  0.6 0.0 copy-start.1
  0.6 0.0 copy-start
  0.7 45.2 %shard_map.155 = (bf16[128,512]{1,0:T(8,128)(2,1)S(1)}, bf16[128,512]{1,0:T(8,128)(2,1)S(1)}, bf16[32,16,128]{2,1,0:T(8,128)(2,1)S(1)}, bf16[32,16,128]{2,1,0:T(8,128)(2,1)S(1)}) custom-call(bf16[128,512]{1,0:T(8,128)(2,1)} %q_hbm.1, bf16[128,512]{1,0:T(8,128)(2,1)} %k_hbm.3, bf16[128,512]{1,0:T(8,128)(2,1)} %v_hbm.3, bf16[128,512]{1,0:T(8,128)(2,1)} %h_hbm.1, ...), custom_call_target="tpu_custom_call" | custom-call | tf_op jit(solution)/shard_map/pallas_call | solution.py:435
  45.9 0.0 copy-done.1
  45.9 0.0 copy-done
  45.9 1.3 %shard_map.156 = (bf16[128,512]{1,0:T(8,128)(2,1)}, bf16[128,512]{1,0:T(8,128)(2,1)}, bf16[128,512]{1,0:T(8,128)(2,1)}, bf16[128,512]{1,0:T(8,128)(2,1)}, f32[128,512]{1,0:T(8,128)}) custom-call(bf16[128,512]{1,0:T(8,128)(2,1)S(1)} %get-tuple-element.9.mixed_in, bf16[128,512]{1,0:T(8,128)(2,1)S(1)} %get-tuple-element.10.qg_in, ...), custom_call_target="tpu_custom_call" | custom-call | tf_op jit(solution)/shard_map/pallas_call | solution.py:477
Async XLA Ops:
  0.6 45.2 %copy-start.1 = (bf16[128,512]{1,0:T(8,128)(2,1)S(1)}, bf16[128,512]{1,0:T(8,128)(2,1)}, u32[]{:S(2)}) copy-start(bf16[128,512]{1,0:T(8,128)(2,1)} %v_hbm.3) | copy-start | bytes 393220
  0.6 45.2 %copy-start = (bf16[128,512]{1,0:T(8,128)(2,1)S(1)}, bf16[128,512]{1,0:T(8,128)(2,1)}, u32[]{:S(2)}) copy-start(bf16[128,512]{1,0:T(8,128)(2,1)} %k_hbm.3) | copy-start | bytes 393220
